TPU v7x, 32 devices: a whole 2x2x4 slice. The times are simulated.
32 devices in a mesh: img: 8 (over z, y), grp: 4 (over x, core).
Axes of the slice: x: 2, y: 2, z: 4, core: 2. Of those that a mesh axis runs over, the one named last changes fastest.
Arguments:
- images: bfloat16 [12288, 9216], P(('img', 'grp')), may hold values from -64 to 64, as said below
- expansion_basis: bfloat16 [9216, 960], P(None, 'img'), may hold values from -0.0625 to 0.0625
- block_sizes: int32 [16], replicated, may hold values from 1 to 80, 480 in all
- keep_count: int32 [16], replicated, may hold values from 1 to 8
- start_block: float32 [16, 80, 8], replicated, may hold values from -6 to 6
Outputs:
- features: float32 [12288, 256], P(('img', 'grp'))
- values: float32 [16, 8], replicated
Inputs may be any that keep to these rules, and one draw needn't show every extreme that they name: `images`: pixel values of order one. `block_sizes`: the 16 sizes sum to 480.
All inputs are finite; a program needn't handle non-finite values.
Results may differ from a plain program's by a relative error of at most 0.025.
Values may be sent and summed in bfloat16 or wider, within the bound.
No kernel may reach another device: no remote copies, remote signals or barrier semaphores. Data moves between devices by JAX's collectives and lax.ppermute only.
A program may use at most 128 MiB of HBM per device.

v0:
```python
import jax
import jax.numpy as jnp
from jax import lax
from jax.sharding import PartitionSpec as P

NMAX = 80
L = 16
S = 480
KMAX = 8
ITERS = 3
HIGH = lax.Precision.HIGHEST


def selector(block_sizes, total, count, width):
    offsets = jnp.cumsum(block_sizes) - block_sizes
    column = jnp.arange(total, dtype=jnp.int32)[:, None, None]
    inside = jnp.arange(width, dtype=jnp.int32)[None, None, :]
    hit = (column == offsets[None, :, None] + inside) & (inside < block_sizes[None, :, None])
    return hit.astype(jnp.bfloat16).reshape(total, count * width)


def subspace(cover, block_sizes, keep_count, start_block):
    width = cover.shape[1]
    ranks = start_block.shape[2]
    inside = jnp.arange(width, dtype=jnp.int32)[None, :, None] < block_sizes[:, None, None]
    keep = jnp.minimum(keep_count, (block_sizes + 1) // 2)
    current = jnp.where(inside, start_block, jnp.zeros_like(start_block))
    for turn in range(ITERS):
        product = jnp.einsum("bij,bjk->bik", cover, current, precision=HIGH)
        columns = []
        for column_id in range(ranks):
            vector = product[:, :, column_id]
            for earlier in columns:
                vector = vector - jnp.sum(earlier * vector, axis=1, keepdims=True) * earlier
            length = jnp.sqrt(jnp.sum(vector * vector, axis=1, keepdims=True))
            alive = (column_id < keep)[:, None]
            columns.append(jnp.where(alive, vector / length, jnp.zeros_like(vector)))
        current = jnp.stack(columns, axis=2)
    product = jnp.einsum("bij,bjk->bik", cover, current, precision=HIGH)
    found = jnp.sum(current * product, axis=1)
    return (current, found)


def spread(partial_value, block_sizes, keep_count, start_block, owners, owner):
    slots = -(-partial_value.shape[0] // owners)
    extra = slots * owners - partial_value.shape[0]
    stacked = jnp.pad(partial_value, ((0, extra), (0, 0), (0, 0)))
    first = owner * slots
    mine_sizes = lax.dynamic_slice_in_dim(jnp.pad(block_sizes, (0, extra)), first, slots)
    mine_keep = lax.dynamic_slice_in_dim(jnp.pad(keep_count, (0, extra)), first, slots)
    mine_start = lax.dynamic_slice_in_dim(
        jnp.pad(start_block, ((0, extra), (0, 0), (0, 0))), first, slots
    )
    return (stacked, mine_sizes, mine_keep, mine_start)


def per_device(images, expansion_basis, block_sizes, keep_count, start_block):
    rows = images.shape[0]
    coeffs = jnp.dot(
        images,
        lax.all_gather(expansion_basis, "img", axis=1, tiled=True),
        preferred_element_type=jnp.float32,
    ).astype(jnp.bfloat16)
    samples = coeffs.reshape(2 * rows, S)
    pick = selector(block_sizes, S, L, NMAX)
    padded = jnp.dot(samples, pick, preferred_element_type=jnp.float32).astype(jnp.bfloat16)
    wide = padded.reshape(2 * rows, L, NMAX)
    scale = 1.0 / (2 * rows * lax.axis_size("img") * lax.axis_size("grp"))
    partial_value = (
        jnp.einsum("rli,rlj->lij", wide, wide, preferred_element_type=jnp.float32) * scale
    )
    stacked, mine_sizes, mine_keep, mine_start = spread(
        partial_value,
        block_sizes,
        keep_count,
        start_block,
        lax.axis_size(("img", "grp")),
        lax.axis_index(("img", "grp")),
    )
    owned = lax.psum_scatter(stacked, ("img", "grp"), scatter_dimension=0, tiled=True)
    solved, quotients = subspace(owned, mine_sizes, mine_keep, mine_start)
    vectors, found = (
        lax.all_gather(solved, ("img", "grp"), axis=0, tiled=True),
        lax.all_gather(quotients, ("img", "grp"), axis=0, tiled=True),
    )
    vectors = vectors[:L]
    found = found[:L]
    rounded = vectors.astype(jnp.bfloat16)
    features = jnp.einsum("rli,lij->rlj", wide, rounded, preferred_element_type=jnp.float32)
    return (features.reshape(rows, 2 * L * KMAX), found)


def solution(mesh):
    in_specs = (P(("img", "grp"), None), P(None, "img"), P(), P(), P())
    out_specs = (P(("img", "grp"), None), P())
    return jax.shard_map(
        per_device, mesh=mesh, in_specs=in_specs, out_specs=out_specs, check_vma=False
    )
```

profile of v0, /device:TPU:14, one launch (start us, length us, event | category | flops | bytes accessed | tf_op | source)
XLA Modules:
  0.0 784.9 jit_solution(9824263346163303519)
XLA Ops:
  7.2 0.7 all-gather.3.cloned.1.call-update
  8.6 341.4 %all-gather.3.cloned.1.call-done = bf16[9216,960]{0,1:T(8,128)(2,1)} async-done(((bf16[9216,120]{0,1:T(8,128)(2,1)}), bf16[9216,960]{0,1:T(8,128)(2,1)}) %all-gather.3.cloned.1.call-update) | async-done | bytes 17694736 | tf_op jit(solution)/shard_map/all_gather | solution.py:61
  350.0 15.1 %convolution_convert_fusion.1 = bf16[384,960]{0,1:T(8,128)(2,1)S(1)} fusion(bf16[384,9216]{1,0:T(8,128)(2,1)} %param.5, bf16[9216,960]{0,1:T(8,128)(2,1)} %all-gather.3.cloned.1.call-done), kind=kOutput, calls=%fused_computation.3 | convolution fusion | flops 6795141120 | bytes 25509888 | tf_op jit(solution)/shard_map/dot_general | solution.py:59
  365.9 2.5 convolution_convert_fusion
  368.5 2.7 copy.19
  371.2 0.7 convolution_multiply_fusion
  371.9 1.1 pad.17
  382.0 0.7 iota_compare_fusion.1
  382.7 96.0 %reduce-scatter.2.cloned.1.call-done = f32[1,80,80]{2,1,0:T(8,128)} async-done(((f32[32,80,80]{2,1,0:T(8,128)}), f32[1,80,80]{2,1,0:T(8,128)}) %reduce-scatter.2.cloned.1.call-update) | async-done | bytes 25616 | tf_op jit(solution)/shard_map/reduce_scatter | solution.py:80
  478.7 0.9 convolution_bitcast_fusion.3
  479.6 0.6 multiply_reduce_fusion.86
  480.9 0.6 fusion.37
  481.6 1.3 fusion.31
  483.6 2.0 multiply_reduce_fusion.84
  485.5 4.4 multiply_reduce_fusion.64
  490.6 4.4 multiply_reduce_fusion.63
  495.0 1.9 multiply_reduce_fusion.80
  497.6 1.9 multiply_reduce_fusion.77
  499.5 5.0 multiply_reduce_fusion.62
  505.2 3.2 multiply_reduce_fusion.61
  508.4 1.9 multiply_reduce_fusion.71
  511.0 1.7 multiply_reduce_fusion.66
  512.7 2.6 multiply_reduce_fusion.60
  516.0 1.9 multiply_reduce_fusion.59
  517.9 1.9 multiply_reduce_fusion.58
  520.5 17.5 %broadcast_select_fusion.5 = (f32[1,80,1]{1,2,0:T(1,128)S(1)}, f32[1,80,1]{1,2,0:T(1,128)S(1)}, f32[1,80,1]{1,2,0:T(1,128)S(1)}, f32[1,80,1]{1,2,0:T(1,128)S(1)}...) fusion(pred[]{:T(512)} %bitcast.20, f32[1,80,1]{1,2,0:T(1,128)S(1)} %get-tuple-element.193, ...), kind=kLoop, calls=%fused_computation.33 | loop fusion | flops 5600 | bytes 4947 | tf_op jit(solution)/shard_map/jit(_where)/select_n | solution.py:37
  538.1 0.9 convolution_bitcast_fusion.2
  539.0 0.6 multiply_reduce_fusion.57
  540.3 0.6 fusion.30
  540.9 1.3 fusion.24
  542.9 2.0 multiply_reduce_fusion.55
  544.9 4.4 multiply_reduce_fusion.35
  549.9 4.4 multiply_reduce_fusion.34
  554.3 1.9 multiply_reduce_fusion.51
  556.9 1.9 multiply_reduce_fusion.48
  558.8 5.0 multiply_reduce_fusion.33
  564.6 3.2 multiply_reduce_fusion.32
  567.7 1.9 multiply_reduce_fusion.42
  570.4 1.7 multiply_reduce_fusion.37
  572.1 2.6 multiply_reduce_fusion.31
  575.4 1.9 multiply_reduce_fusion.30
  577.3 1.9 multiply_reduce_fusion.29
  579.9 17.5 %broadcast_select_fusion.4 = (f32[1,80,1]{1,2,0:T(1,128)S(1)}, f32[1,80,1]{1,2,0:T(1,128)S(1)}, f32[1,80,1]{1,2,0:T(1,128)S(1)}, f32[1,80,1]{1,2,0:T(1,128)S(1)}...) fusion(pred[]{:T(512)} %bitcast.20, f32[1,80,1]{1,2,0:T(1,128)S(1)} %get-tuple-element.158, ...), kind=kLoop, calls=%fused_computation.32 | loop fusion | flops 5600 | bytes 4947 | tf_op jit(solution)/shard_map/jit(_where)/select_n | solution.py:37
  597.4 0.9 convolution_bitcast_fusion.1
  598.4 0.6 multiply_reduce_fusion.28
  600.3 1.3 fusion.17
  602.3 2.0 multiply_reduce_fusion.26
  604.3 4.4 multiply_reduce_fusion.6
  609.3 4.4 multiply_reduce_fusion.5
  613.7 1.9 multiply_reduce_fusion.22
  616.3 1.9 multiply_reduce_fusion.19
  618.2 5.0 multiply_reduce_fusion.4
  623.9 3.2 multiply_reduce_fusion.3
  627.1 1.9 multiply_reduce_fusion.13
  629.7 1.7 multiply_reduce_fusion.8
  631.5 2.6 multiply_reduce_fusion.2
  634.8 1.9 multiply_reduce_fusion.1
  636.6 1.9 multiply_reduce_fusion
  639.3 17.5 %broadcast_select_fusion.3 = (f32[1,80,1]{1,2,0:T(1,128)S(1)}, f32[1,80,1]{1,2,0:T(1,128)S(1)}, f32[1,80,1]{1,2,0:T(1,128)S(1)}, f32[1,80,1]{1,2,0:T(1,128)S(1)}...) fusion(pred[]{:T(512)} %bitcast.20, f32[1,80,1]{1,2,0:T(1,128)S(1)} %get-tuple-element.123, ...), kind=kLoop, calls=%fused_computation.31 | loop fusion | flops 5600 | bytes 4947 | tf_op jit(solution)/shard_map/jit(_where)/select_n | solution.py:37
  656.8 59.5 %all_gather.10 = bf16[32,80,8]{1,2,0:T(8,128)(2,1)S(1)} all-gather(bf16[1,80,8]{1,2,0:T(8,128)(2,1)S(1)} %convert.6), channel_id=1, replica_groups=mesh['img'=8,'grp'=4] {'img','grp'}, dimensions={0}, use_global_device_ids=true | all-gather | bytes 42240 | tf_op jit(solution)/shard_map/all_gather | solution.py:83
  716.6 4.9 copy.20
  721.5 6.3 reshape.4100
  728.4 48.9 %all-reduce.4 = f32[256]{0:T(256)S(1)} all-reduce(f32[256]{0:T(256)S(1)} %dynamic-update-slice), channel_id=2, replica_groups=mesh['img'=8,'grp'=4] {'img','grp'}, use_global_device_ids=true, to_apply=%add.4 | all-reduce | flops 256 | bytes 2048
  777.4 0.7 copy.21
  (38 shorter events, 4.4 us)
Async XLA Ops:
  7.2 0.8 copy-start.2
  7.2 342.9 %all-gather.3.cloned.1.call-start = ((), (), s32[]{:S(2)}) async-start(), calls=%async_computation.1 | async-start | bytes 19906560 | tf_op jit(solution)/shard_map/all_gather | solution.py:61
  7.9 470.8 %reduce-scatter.2.cloned.1.call-start = ((), (), s32[]{:S(2)}) async-start(), calls=%async_computation.2 | async-start | bytes 1351680 | tf_op jit(solution)/shard_map/reduce_scatter | solution.py:80
  371.8 4.4 copy-start.3
  371.8 106.8 %copy-start.1 = (f32[16,80,8]{1,2,0:T(8,128)S(1)}, f32[16,80,8]{1,2,0:T(8,128)}, u32[]{:S(2)}) copy-start(f32[16,80,8]{1,2,0:T(8,128)} %param.9) | copy-start | bytes 122884
  721.5 6.3 copy-start
Sparse Core Ops, SparseCore 0:
  9.5 340.4 all-gather.2
  373.1 105.4 reduce-scatter.1
where the time goes:
time: 788 us; the launch traced here: 785 us
  waiting for transfers between devices  438 us (56%)
  other arithmetic  161 us (20%)
  blocking collectives  108 us (14%)
  between operations  38.6 us (5%)
  matrix products  21.7 us (3%)
  local copies, waits for them, and re-layouts  17.4 us (2%)
    all_gather x1, waiting for transfers between devices, per_device(): lax.all_gather(expansion_basis, 'img', axis=1, tiled=True)  341 us
    reduce_scatter x1, waiting for transfers between devices, per_device(): lax.psum_scatter(stacked, ('img', 'grp'), scatter_dimension=0, tiled=True)  96 us
    reduce_sum x33, other arithmetic, subspace(): vector = vector - jnp.sum(earlier * vector, axis=1, keepdims=True) * earlier  86.9 us
    all_gather x1, blocking collectives, per_device(): lax.all_gather(solved, ('img', 'grp'), axis=0, tiled=True)  59.5 us
    select_n x3, other arithmetic, subspace(): columns.append(jnp.where(alive, vector / length, jnp.zeros_like(vector)))  52.4 us
    unnamed x1, blocking collectives  48.9 us
    reduce_sum x12, other arithmetic, subspace(): length = jnp.sqrt(jnp.sum(vector * vector, axis=1, keepdims=True))  19.3 us
  transfers between devices with their start and end apart: 2, of which 2 were waited for; matrix products, arithmetic and copies ran while one was open for 0% of the time, Pallas kernels for 0%

commit v1 on v0

--- a/solution.py
+++ b/solution.py
@@ -9,6 +9,28 @@
 KMAX = 8
 ITERS = 3
 HIGH = lax.Precision.HIGHEST
+
+
+def in_order(blocks, dim):
+    shape = list(blocks.shape[1:])
+    shape[dim] *= blocks.shape[0]
+    return jnp.moveaxis(blocks, 0, dim).reshape(shape)
+
+
+def collect(shard, axis, dim):
+    size = lax.axis_size(axis)
+    pairs = [(i, (i + 1) % size) for i in range(size)]
+    back = [(b, a) for a, b in pairs]
+    lower, upper = ([], [])
+    for step in range(size - 1):
+        if step % 2 == 0:
+            lower.append(lax.ppermute(lower[-1] if lower else shard, axis, pairs))
+        else:
+            upper.append(lax.ppermute(upper[-1] if upper else shard, axis, back))
+    blocks = jnp.stack([*lower[::-1], shard, *upper])
+    shift = lax.axis_index(axis) - len(lower)
+    blocks = blocks[(jnp.arange(size) - shift) % size]
+    return in_order(blocks, dim)
 
 
 def selector(block_sizes, total, count, width):
@@ -57,9 +79,7 @@
 def per_device(images, expansion_basis, block_sizes, keep_count, start_block):
     rows = images.shape[0]
     coeffs = jnp.dot(
-        images,
-        lax.all_gather(expansion_basis, "img", axis=1, tiled=True),
-        preferred_element_type=jnp.float32,
+        images, collect(expansion_basis, "img", 1), preferred_element_type=jnp.float32
     ).astype(jnp.bfloat16)
     samples = coeffs.reshape(2 * rows, S)
     pick = selector(block_sizes, S, L, NMAX)

time: 788 us -> 829 us (1.052)
  local copies, waits for them, and re-layouts: 17.4 us -> 50.8 us
  waiting for transfers between devices: 438 us -> 423 us
  other arithmetic: 161 us -> 175 us
    all_gather x1 -> x0, waiting for transfers between devices: 341 us -> none  [per_device(): lax.all_gather(expansion_basis, 'img', axis=1, tiled=True)]
    ppermute x0 -> x7, waiting for transfers between devices: none -> 327 us  [the longest x4 327 us: collect(): lower.append(lax.ppermute(lower[-1] if lower else shard, axis, pairs))]
    gather x0 -> x3, local copies, waits for them, and re-layouts: none -> 23.2 us  [collect(): blocks = blocks[(jnp.arange(size) - shift) % size]]
    unnamed x1 -> x2, other arithmetic: 0.01 us -> 14.2 us
    unnamed x11 -> x24, local copies, waits for them, and re-layouts: 0.94 us -> 9.82 us
  transfers between devices with their start and end apart: 2 -> 8, of which waited for: 2 -> 5; matrix products, arithmetic and copies ran while one was open for 0% -> 1% of each run, Pallas kernels for 0% -> 0%
where the time goes in v1:
time: 829 us; the launch traced here: 827 us
  waiting for transfers between devices  423 us (51%)
  other arithmetic  175 us (21%)
  blocking collectives  108 us (13%)
  local copies, waits for them, and re-layouts  50.8 us (6%)
  between operations  38.7 us (5%)
  matrix products  21.8 us (3%)
    ppermute x4, waiting for transfers between devices, collect(): lower.append(lax.ppermute(lower[-1] if lower else shard, axis, pairs))  327 us
    reduce_scatter x1, waiting for transfers between devices, per_device(): lax.psum_scatter(stacked, ('img', 'grp'), scatter_dimension=0, tiled=True)  96.5 us
    reduce_sum x33, other arithmetic, subspace(): vector = vector - jnp.sum(earlier * vector, axis=1, keepdims=True) * earlier  86.9 us
    all_gather x1, blocking collectives, per_device(): lax.all_gather(solved, ('img', 'grp'), axis=0, tiled=True)  59.5 us
    select_n x3, other arithmetic, subspace(): columns.append(jnp.where(alive, vector / length, jnp.zeros_like(vector)))  52.4 us
    unnamed x1, blocking collectives  48.9 us
    gather x3, local copies, waits for them, and re-layouts, collect(): blocks = blocks[(jnp.arange(size) - shift) % size]  23.2 us
    reduce_sum x12, other arithmetic, subspace(): length = jnp.sqrt(jnp.sum(vector * vector, axis=1, keepdims=True))  19.3 us
  transfers between devices with their start and end apart: 8, of which 5 were waited for; matrix products, arithmetic and copies ran while one was open for 1% of the time, Pallas kernels for 0%

profile of v1, /device:TPU:14, one launch (start us, length us, event | category | flops | bytes accessed | tf_op | source)
XLA Modules:
  0.0 826.5 jit_solution(2463675826139420620)
XLA Ops:
  7.2 1.6 collective-permute-start
  8.8 48.5 %collective-permute-done = bf16[9216,120]{0,1:T(8,128)(2,1)S(1)} collective-permute-done((bf16[9216,120]{0,1:T(8,128)(2,1)}, bf16[9216,120]{0,1:T(8,128)(2,1)S(1)}, u32[]{:S(2)}, u32[]{:S(2)}) %collective-permute-start) | collective-permute-done | bytes 2211872 | tf_op jit(solution)/shard_map/ppermute | solution.py:27
  57.3 2.4 collective-permute-start.1
  59.7 93.9 %collective-permute-done.1 = bf16[9216,120]{0,1:T(8,128)(2,1)S(1)} collective-permute-done((bf16[9216,120]{0,1:T(8,128)(2,1)S(1)}, bf16[9216,120]{0,1:T(8,128)(2,1)S(1)}, u32[]{:S(2)}, u32[]{:S(2)}) %collective-permute-start.1) | collective-permute-done | bytes 2211872 | tf_op jit(solution)/shard_map/ppermute | solution.py:27
  153.7 1.3 copy-done.1
  155.6 1.5 collective-permute-start.5
  157.1 93.6 %collective-permute-done.2 = bf16[9216,120]{0,1:T(8,128)(2,1)} collective-permute-done((bf16[9216,120]{0,1:T(8,128)(2,1)S(1)}, bf16[9216,120]{0,1:T(8,128)(2,1)}, u32[]{:S(2)}, u32[]{:S(2)}) %collective-permute-start.2) | collective-permute-done | bytes 2211872 | tf_op jit(solution)/shard_map/ppermute | solution.py:27
  253.7 1.6 collective-permute-start.6
  255.4 90.6 %collective-permute-done.3 = bf16[9216,120]{0,1:T(8,128)(2,1)} collective-permute-done((bf16[9216,120]{0,1:T(8,128)(2,1)}, bf16[9216,120]{0,1:T(8,128)(2,1)}, u32[]{:S(2)}, u32[]{:S(2)}) %collective-permute-start.3) | collective-permute-done | bytes 2211872 | tf_op jit(solution)/shard_map/ppermute | solution.py:27
  345.9 1.8 bitcast_dynamic-update-slice_fusion.7
  347.7 1.8 bitcast_dynamic-update-slice_fusion.6
  350.0 1.8 bitcast_dynamic-update-slice_fusion.2
  351.7 1.8 bitcast_dynamic-update-slice_fusion.1
  353.7 6.3 fusion.43
  360.0 8.5 %gather_fusion.1 = bf16[8,4608,120]{1,2,0:T(8,128)(2,1)} fusion(bf16[8,4608,120]{1,2,0:T(8,128)(2,1)} %get-tuple-element.195, s32[1024]{0:T(1024)S(1)} %pad_clamp_fusion), kind=kCustom, calls=%fused_computation.1 | custom fusion | bytes 17694752 | tf_op jit(solution)/shard_map/gather | solution.py:32
  368.5 8.4 %gather_fusion = bf16[8,4608,120]{1,2,0:T(8,128)(2,1)} fusion(bf16[8,4608,120]{1,2,0:T(8,128)(2,1)} %get-tuple-element.194, s32[1024]{0:T(1024)S(1)} %pad_clamp_fusion), kind=kCustom, calls=%fused_computation | custom fusion | bytes 17694752 | tf_op jit(solution)/shard_map/gather | solution.py:32
  376.8 14.2 %pad_maximum_fusion = bf16[8,9216,120]{1,2,0:T(8,128)(2,1)} fusion(bf16[8,4608,120]{1,2,0:T(8,128)(2,1)} %gather_fusion.1, bf16[8,4608,120]{1,2,0:T(8,128)(2,1)} %gather_fusion), kind=kLoop, calls=%fused_computation.2 | loop fusion | flops 35389440 | bytes 35389440
  391.0 15.0 %fusion.2 = bf16[384,960]{0,1:T(8,128)(2,1)S(1)} fusion(bf16[9216,960]{0,1:T(8,128)(2,1)} %bitcast.336, bf16[384,9216]{1,0:T(8,128)(2,1)} %param.5), kind=kOutput, calls=%fused_computation.15 | convolution fusion | flops 6795141120 | bytes 25509888 | tf_op jit(solution)/shard_map/dot_general | solution.py:81
  406.9 2.5 convolution_convert_fusion
  409.4 2.7 copy.19
  423.6 96.5 %reduce-scatter.2.cloned.1.call-done = f32[1,80,80]{2,1,0:T(8,128)} async-done(((f32[32,80,80]{2,1,0:T(8,128)}), f32[1,80,80]{2,1,0:T(8,128)}) %reduce-scatter.2.cloned.1.call-update) | async-done | bytes 25616 | tf_op jit(solution)/shard_map/reduce_scatter | solution.py:100
  525.1 2.0 multiply_reduce_fusion.84
  527.0 4.4 multiply_reduce_fusion.64
  532.1 4.4 multiply_reduce_fusion.63
  536.5 1.9 multiply_reduce_fusion.80
  539.1 1.9 multiply_reduce_fusion.77
  541.0 5.0 multiply_reduce_fusion.62
  546.7 3.2 multiply_reduce_fusion.61
  549.9 1.9 multiply_reduce_fusion.71
  552.5 1.7 multiply_reduce_fusion.66
  554.3 2.6 multiply_reduce_fusion.60
  557.6 1.9 multiply_reduce_fusion.59
  559.4 1.9 multiply_reduce_fusion.58
  562.1 17.5 %broadcast_select_fusion.5 = (f32[1,80,1]{1,2,0:T(1,128)S(1)}, f32[1,80,1]{1,2,0:T(1,128)S(1)}, f32[1,80,1]{1,2,0:T(1,128)S(1)}, f32[1,80,1]{1,2,0:T(1,128)S(1)}...) fusion(pred[]{:T(512)} %bitcast.32, f32[1,80,1]{1,2,0:T(1,128)S(1)} %get-tuple-element.193, ...), kind=kLoop, calls=%fused_computation.50 | loop fusion | flops 5600 | bytes 4947 | tf_op jit(solution)/shard_map/jit(_where)/select_n | solution.py:59
  584.5 2.0 multiply_reduce_fusion.55
  586.4 4.4 multiply_reduce_fusion.35
  591.5 4.4 multiply_reduce_fusion.34
  595.9 1.9 multiply_reduce_fusion.51
  598.5 1.9 multiply_reduce_fusion.48
  600.4 5.0 multiply_reduce_fusion.33
  606.1 3.2 multiply_reduce_fusion.32
  609.3 1.9 multiply_reduce_fusion.42
  611.9 1.7 multiply_reduce_fusion.37
  613.6 2.6 multiply_reduce_fusion.31
  616.9 1.9 multiply_reduce_fusion.30
  618.8 1.9 multiply_reduce_fusion.29
  621.5 17.5 %broadcast_select_fusion.4 = (f32[1,80,1]{1,2,0:T(1,128)S(1)}, f32[1,80,1]{1,2,0:T(1,128)S(1)}, f32[1,80,1]{1,2,0:T(1,128)S(1)}, f32[1,80,1]{1,2,0:T(1,128)S(1)}...) fusion(pred[]{:T(512)} %bitcast.32, f32[1,80,1]{1,2,0:T(1,128)S(1)} %get-tuple-element.158, ...), kind=kLoop, calls=%fused_computation.49 | loop fusion | flops 5600 | bytes 4947 | tf_op jit(solution)/shard_map/jit(_where)/select_n | solution.py:59
  643.8 2.0 multiply_reduce_fusion.26
  645.8 4.4 multiply_reduce_fusion.6
  650.8 4.4 multiply_reduce_fusion.5
  655.2 1.9 multiply_reduce_fusion.22
  657.8 1.9 multiply_reduce_fusion.19
  659.7 5.0 multiply_reduce_fusion.4
  665.5 3.2 multiply_reduce_fusion.3
  668.6 1.9 multiply_reduce_fusion.13
  671.3 1.7 multiply_reduce_fusion.8
  673.0 2.6 multiply_reduce_fusion.2
  676.3 1.9 multiply_reduce_fusion.1
  678.2 1.9 multiply_reduce_fusion
  680.8 17.5 %broadcast_select_fusion.3 = (f32[1,80,1]{1,2,0:T(1,128)S(1)}, f32[1,80,1]{1,2,0:T(1,128)S(1)}, f32[1,80,1]{1,2,0:T(1,128)S(1)}, f32[1,80,1]{1,2,0:T(1,128)S(1)}...) fusion(pred[]{:T(512)} %bitcast.32, f32[1,80,1]{1,2,0:T(1,128)S(1)} %get-tuple-element.123, ...), kind=kLoop, calls=%fused_computation.48 | loop fusion | flops 5600 | bytes 4947 | tf_op jit(solution)/shard_map/jit(_where)/select_n | solution.py:59
  698.3 59.5 %all_gather.6 = bf16[32,80,8]{1,2,0:T(8,128)(2,1)S(1)} all-gather(bf16[1,80,8]{1,2,0:T(8,128)(2,1)S(1)} %convert.8), channel_id=1, replica_groups=mesh['img'=8,'grp'=4] {'img','grp'}, dimensions={0}, use_global_device_ids=true | all-gather | bytes 42240 | tf_op jit(solution)/shard_map/all_gather | solution.py:103
  758.3 4.9 copy.20
  763.1 6.3 reshape.4153
  770.0 48.9 %all-reduce.4 = f32[256]{0:T(256)S(1)} all-reduce(f32[256]{0:T(256)S(1)} %dynamic-update-slice), channel_id=2, replica_groups=mesh['img'=8,'grp'=4] {'img','grp'}, use_global_device_ids=true, to_apply=%add.4 | all-reduce | flops 256 | bytes 2048
  (69 shorter events, 21.1 us)
Async XLA Ops:
  7.2 513.0 %reduce-scatter.2.cloned.1.call-start = ((), (), s32[]{:S(2)}) async-start(), calls=%async_computation.1 | async-start | bytes 1351680 | tf_op jit(solution)/shard_map/reduce_scatter | solution.py:100
  7.2 50.1 %collective-permute-start = (bf16[9216,120]{0,1:T(8,128)(2,1)}, bf16[9216,120]{0,1:T(8,128)(2,1)S(1)}, u32[]{:S(2)}, u32[]{:S(2)}) collective-permute-start(bf16[9216,120]{0,1:T(8,128)(2,1)} %param.6), channel_id=1, source_target_pairs={{0,4},{4,8},{8,12},{12,16},{16,20},{20,24},{24,28},{28,0},{1,5},{5... | collective-permute-start | bytes 6635528 | tf_op jit(solution)/shard_map/ppermute | solution.py:27
  57.3 96.4 %collective-permute-start.1 = (bf16[9216,120]{0,1:T(8,128)(2,1)S(1)}, bf16[9216,120]{0,1:T(8,128)(2,1)S(1)}, u32[]{:S(2)}, u32[]{:S(2)}) collective-permute-start(bf16[9216,120]{0,1:T(8,128)(2,1)S(1)} %collective-permute-done), channel_id=1, source_target_pairs={{0,4},{4,8},{8,12},{12,16},{16,20},{20,24},{24,28},{28,0},{1,5},{5... | collective-permute-start | bytes 6635528 | tf_op jit(solution)/shard_map/ppermute | solution.py:27
  59.7 95.9 %collective-permute-start.4 = (bf16[9216,120]{0,1:T(8,128)(2,1)}, bf16[9216,120]{0,1:T(8,128)(2,1)}, u32[]{:S(2)}, u32[]{:S(2)}) collective-permute-start(bf16[9216,120]{0,1:T(8,128)(2,1)} %param.6), channel_id=1, source_target_pairs={{4,0},{8,4},{12,8},{16,12},{20,16},{24,20},{28,24},{0,28},{5,1},{9... | collective-permute-start | bytes 6635528 | tf_op jit(solution)/shard_map/ppermute | solution.py:29
  153.7 1.4 copy-start.1
  155.0 95.6 %collective-permute-start.2 = (bf16[9216,120]{0,1:T(8,128)(2,1)S(1)}, bf16[9216,120]{0,1:T(8,128)(2,1)}, u32[]{:S(2)}, u32[]{:S(2)}) collective-permute-start(bf16[9216,120]{0,1:T(8,128)(2,1)S(1)} %collective-permute-done.1), channel_id=1, source_target_pairs={{0,4},{4,8},{8,12},{12,16},{16,20},{20,24},{24,28},{28,0},{1,5},{5... | collective-permute-start | bytes 6635528 | tf_op jit(solution)/shard_map/ppermute | solution.py:27
  155.6 98.1 %collective-permute-start.5 = (bf16[9216,120]{0,1:T(8,128)(2,1)}, bf16[9216,120]{0,1:T(8,128)(2,1)}, u32[]{:S(2)}, u32[]{:S(2)}) collective-permute-start(bf16[9216,120]{0,1:T(8,128)(2,1)} %collective-permute-done.4), channel_id=1, source_target_pairs={{4,0},{8,4},{12,8},{16,12},{20,16},{24,20},{28,24},{0,28},{5,1},{9... | collective-permute-start | bytes 6635528 | tf_op jit(solution)/shard_map/ppermute | solution.py:29
  250.6 95.3 %collective-permute-start.3 = (bf16[9216,120]{0,1:T(8,128)(2,1)}, bf16[9216,120]{0,1:T(8,128)(2,1)}, u32[]{:S(2)}, u32[]{:S(2)}) collective-permute-start(bf16[9216,120]{0,1:T(8,128)(2,1)} %collective-permute-done.2), channel_id=1, source_target_pairs={{0,4},{4,8},{8,12},{12,16},{16,20},{20,24},{24,28},{28,0},{1,5},{5... | collective-permute-start | bytes 6635528 | tf_op jit(solution)/shard_map/ppermute | solution.py:27
  253.7 95.8 %copy-start.2 = (bf16[9216,120]{0,1:T(8,128)(2,1)S(1)}, bf16[9216,120]{0,1:T(8,128)(2,1)}, u32[]{:S(2)}) copy-start(bf16[9216,120]{0,1:T(8,128)(2,1)} %copy-done.1) | copy-start | bytes 6635524
  253.7 96.1 %copy-start = (bf16[9216,120]{0,1:T(8,128)(2,1)S(1)}, bf16[9216,120]{0,1:T(8,128)(2,1)}, u32[]{:S(2)}) copy-start(bf16[9216,120]{0,1:T(8,128)(2,1)} %param.6) | copy-start | bytes 6635524
  253.7 99.8 %collective-permute-start.6 = (bf16[9216,120]{0,1:T(8,128)(2,1)}, bf16[9216,120]{0,1:T(8,128)(2,1)S(1)}, u32[]{:S(2)}, u32[]{:S(2)}) collective-permute-start(bf16[9216,120]{0,1:T(8,128)(2,1)} %collective-permute-done.5), channel_id=1, source_target_pairs={{4,0},{8,4},{12,8},{16,12},{20,16},{24,20},{28,24},{0,28},{5,1},{9... | collective-permute-start | bytes 6635528 | tf_op jit(solution)/shard_map/ppermute | solution.py:29
  406.9 7.1 copy-start.5
  406.9 10.3 %copy-start.6 = (s32[16]{0:T(128)S(1)}, s32[16]{0:T(128)}, u32[]{:S(2)}) copy-start(s32[16]{0:T(128)} %param.8) | copy-start | bytes 196
  406.9 113.3 %copy-start.4 = (f32[16,80,8]{1,2,0:T(8,128)S(1)}, f32[16,80,8]{1,2,0:T(8,128)}, u32[]{:S(2)}) copy-start(f32[16,80,8]{1,2,0:T(8,128)} %param.9) | copy-start | bytes 122884
  520.2 249.3 %copy-start.3 = (f32[1,80,80]{2,1,0:T(8,128)S(1)}, f32[1,80,80]{2,1,0:T(8,128)}, u32[]{:S(2)}) copy-start(f32[1,80,80]{2,1,0:T(8,128)} %reduce-scatter.2.cloned.1.call-done) | copy-start | bytes 76804
Sparse Core Ops, SparseCore 0:
  414.1 106.0 reduce-scatter.1
